TPU v7x, 256 devices: a whole 4x4x8 slice. The times are simulated.
256 devices in a mesh: tensor: 8 (over z), expert: 32 (over x, y, core).
Axes of the slice: x: 4, y: 4, z: 8, core: 2. Of those that a mesh axis runs over, the one named last changes fastest.
Arguments:
- queries: bfloat16 [768, 64, 576], P('expert', 'tensor'), may hold values from -200 to 200
- latent_cache_rows: bfloat16 [768, 24, 576], P('expert'), may hold values from -5 to 5
- lengths: int32 [768], P('expert'), may hold values from 6 to 24, as said below
- value_up_weight: bfloat16 [64, 512, 128], P('tensor'), may hold values from -0.25 to 0.25
- w_output: bfloat16 [8192, 7168], P('tensor', 'expert'), may hold values from -0.0625 to 0.0625
- residual: bfloat16 [768, 7168], P(None, 'expert'), may hold values from -3 to 3
- norm_gain: float32 [7168], replicated, may hold values from 0.1 to 1.9
- routes: int32 [768, 8], replicated, may hold values from 0 to 31, as said below
- gate_values: float32 [768, 8], replicated, may hold values from 0.05 to 0.5
- capacity: int32 [32], replicated, may hold values from 224 to 448, as said below
- w_gate: bfloat16 [32, 7168, 2048], P('expert', None, 'tensor'), may hold values from -0.0625 to 0.0625
- w_up: bfloat16 [32, 7168, 2048], P('expert', None, 'tensor'), may hold values from -0.0625 to 0.0625
- w_down: bfloat16 [32, 2048, 7168], P('expert', 'tensor'), may hold values from -0.125 to 0.125
Outputs:
- layer_output: bfloat16 [768, 7168], P('tensor', 'expert')
Inputs may be any that keep to these rules, and one draw needn't show every extreme that they name: Row r attends over its first lengths[r] cache slots; some row fills all 24 in every draw. `routes`: each row names 8 different experts. Some expert has capacity 448 in every draw.
All inputs are finite; a program needn't handle non-finite values.
Results may differ from a plain program's by a relative error of at most 0.0073.
Values may be sent and summed in bfloat16 or wider, within the bound.
No kernel may reach another device: no remote copies, remote signals or barrier semaphores. Data moves between devices by JAX's collectives and lax.ppermute only.
A program may use at most 128 MiB of HBM per device.

v0:
```python
import jax
import jax.numpy as jnp
from jax import lax
from jax.sharding import PartitionSpec as P

ROTARY_CHANNELS = 64
NOPE = 128
BUFFER_PLACES = 448


epsilon = 1e-06


def pair_targets(routes, capacity, slot_depth, row_total):
    experts_total = capacity.shape[0]
    flat_ids = routes.reshape(-1)
    one_hot = (flat_ids[:, None] == jnp.arange(experts_total, dtype=jnp.int32)[None, :]).astype(
        jnp.int32
    )
    earlier = jnp.cumsum(one_hot, axis=0) - one_hot
    position = jnp.sum(earlier * one_hot, axis=1)
    limit_of = jnp.sum(one_hot * capacity[None, :], axis=1)
    kept_pair = position < limit_of
    target = jnp.where(kept_pair, flat_ids * slot_depth + position, experts_total * slot_depth)
    row_index = jnp.arange(flat_ids.shape[0], dtype=jnp.int32) // routes.shape[1]
    slot_row = (
        jnp.full((experts_total * slot_depth + 1,), row_total, jnp.int32).at[target].set(row_index)
    )
    slot_row = slot_row[: experts_total * slot_depth].reshape(experts_total, slot_depth)
    return (target, slot_row)


def shards(
    queries,
    latent_cache_rows,
    lengths,
    value_up_weight,
    w_output,
    residual,
    norm_gain,
    routes,
    gate_values,
    capacity,
    w_gate,
    w_up,
    w_down,
):
    latent_width = value_up_weight.shape[1]
    softmax_scale = (NOPE + ROTARY_CHANNELS) ** (-0.5)
    scores = (
        jnp.einsum("rhc,rpc->rhp", queries, latent_cache_rows, preferred_element_type=jnp.float32)
        * softmax_scale
    )
    slot_total = latent_cache_rows.shape[1]
    live_slot = lax.broadcasted_iota(jnp.int32, (1, 1, slot_total), 2) < lengths[:, None, None]
    scores = jnp.where(live_slot, scores, -jnp.inf)
    row_peak = jnp.max(scores, axis=-1, keepdims=True)
    weight_exp = jnp.exp(scores - row_peak)
    attention_probs = (weight_exp / jnp.sum(weight_exp, axis=-1, keepdims=True)).astype(
        jnp.bfloat16
    )
    latent_rows = jnp.einsum(
        "onq,oqv->onv",
        attention_probs,
        latent_cache_rows[:, :, :latent_width],
        preferred_element_type=jnp.float32,
    ).astype(jnp.bfloat16)
    head_out = jnp.einsum(
        "rhc,hcv->rhv", latent_rows, value_up_weight, preferred_element_type=jnp.float32
    ).astype(jnp.bfloat16)
    head_rows = head_out.reshape(head_out.shape[0], -1)
    partial_out = jnp.dot(
        lax.all_gather(head_rows, "expert", axis=0, tiled=True),
        w_output,
        preferred_element_type=jnp.float32,
    )
    attention = lax.psum(partial_out, "tensor")
    stream = (residual.astype(jnp.float32) + attention).astype(jnp.bfloat16)
    row_total = stream.shape[0]
    column_width = stream.shape[1]
    target, slot_row = pair_targets(routes, capacity, BUFFER_PLACES, row_total)
    padded = jnp.concatenate([stream, jnp.zeros((1, column_width), jnp.bfloat16)], axis=0)
    outgoing = padded[slot_row]
    incoming = lax.all_to_all(outgoing, "expert", split_axis=0, concat_axis=2, tiled=True)[0]
    as_float = incoming.astype(jnp.float32)
    normed = (
        as_float
        * lax.rsqrt(jnp.mean(as_float * as_float, axis=-1, keepdims=True) + epsilon)
        * norm_gain
    ).astype(jnp.bfloat16)
    gate_pre = jnp.dot(normed, w_gate[0], preferred_element_type=jnp.float32)
    up_pre = jnp.dot(normed, w_up[0], preferred_element_type=jnp.float32)
    activated = (jax.nn.silu(gate_pre) * up_pre).astype(jnp.bfloat16)
    expert_part = jnp.dot(activated, w_down[0], preferred_element_type=jnp.float32)
    sent_back = lax.all_to_all(expert_part[None], "expert", split_axis=2, concat_axis=0, tiled=True)
    back_width = sent_back.shape[-1]
    flat_back = sent_back.reshape(-1, back_width)
    flat_back = jnp.concatenate([flat_back, jnp.zeros((1, back_width), jnp.float32)], axis=0)
    picked = flat_back[target].reshape(routes.shape[0], routes.shape[1], back_width)
    combined = jnp.sum(gate_values[:, :, None] * picked, axis=1)
    tensor_index = lax.axis_index("tensor")
    summed_rows = lax.psum_scatter(combined, "tensor", scatter_dimension=0, tiled=True)
    row_count = summed_rows.shape[0]
    own_rows = lax.dynamic_slice_in_dim(stream, tensor_index * row_count, row_count, 0)
    return (own_rows.astype(jnp.float32) + summed_rows).astype(jnp.bfloat16)


def solution(mesh):
    in_specs = (
        P("expert", "tensor", None),
        P("expert", None, None),
        P("expert"),
        P("tensor", None, None),
        P("tensor", "expert"),
        P(None, "expert"),
        P(),
        P(),
        P(),
        P(),
        P("expert", None, "tensor"),
        P("expert", None, "tensor"),
        P("expert", "tensor", None),
    )
    out_specs = P("tensor", "expert")
    return jax.shard_map(shards, mesh=mesh, in_specs=in_specs, out_specs=out_specs, check_vma=False)
```

profile of v0, /device:TPU:2, one launch (start us, length us, event | category | flops | bytes accessed | tf_op | source)
XLA Modules:
  0.0 760.1 jit_solution(4974229861788617738)
XLA Ops:
  7.4 1.6 fusion.19
  9.2 1.5 convolution_convert_fusion
  13.1 9.4 %reduce-window.6 = s32[32,48,128]{2,1,0:T(8,128)S(1)} reduce-window(s32[32,48,128]{2,1,0:T(8,128)S(1)} %fusion.24, s32[]{:T(128)} %constant.48.clone.1), window={size=1x1x128 pad=0_0x0_0x127_0}, to_apply=%region_3.4 | reduce-window | flops 24969216 | bytes 1572868 | tf_op jit(solution)/shard_map/reduce-window
  24.9 37.6 %all-gather.2.cloned.1.call-done = bf16[768,1024]{1,0:T(8,128)(2,1)} async-done(((bf16[24,1024]{1,0:T(8,128)(2,1)}), bf16[768,1024]{1,0:T(8,128)(2,1)}) %all-gather.2.cloned.1.call-update) | async-done | bytes 1572880 | tf_op jit(solution)/shard_map/all_gather | solution.py:73
  62.4 2.9 fusion.38
  65.4 23.0 %scatter_custom_fusion = s32[14337]{0:T(1024)S(1)} fusion(s32[6144]{0:T(1024)S(1)} %bitcast.79, s32[6144]{0:T(1024)S(1)} %add_select_fusion, s32[]{:T(128)} %constant.49.clone.1), kind=kCustom, calls=%fused_computation.52 | custom fusion | bytes 57352 | tf_op jit(solution)/shard_map/scatter | solution.py:27
  88.6 51.2 %all-reduce.4.cloned.1.call-done = f32[768,224]{0,1:T(8,128)} async-done(((f32[768,224]{0,1:T(8,128)}), f32[768,224]{0,1:T(8,128)}) %all-reduce.4.cloned.1.call-update) | async-done | bytes 688144 | tf_op jit(solution)/shard_map/psum | solution.py:77
  141.3 56.9 %gather_fusion = bf16[14336,224]{1,0:T(8,128)(2,1)} fusion(bf16[769,224]{1,0:T(8,128)(2,1)S(1)} %concatenate.6.clone, s32[14336]{0:T(1024)S(1)} %broadcast_clamp_fusion), kind=kCustom, calls=%fused_computation | custom fusion | bytes 12902400 | tf_op jit(solution)/shard_map/gather | solution.py:83
  198.2 7.6 %all-to-all-start = ((bf16[32,448,224]{2,1,0:T(8,128)(2,1)}), bf16[32,448,224]{2,1,0:T(8,128)(2,1)}, u32[]{:S(2)}, u32[]{:S(2)}) async-start(bf16[32,448,224]{2,1,0:T(8,128)(2,1)} %bitcast.74), calls=%async_computation | async-start | bytes 14680064 | tf_op jit(solution)/shard_map/all_to_all | solution.py:84
  205.9 89.9 %all-to-all-done = bf16[32,448,224]{2,1,0:T(8,128)(2,1)} async-done(((bf16[32,448,224]{2,1,0:T(8,128)(2,1)}), bf16[32,448,224]{2,1,0:T(8,128)(2,1)}, u32[]{:S(2)}, u32[]{:S(2)}) %all-to-all-start) | async-done | bytes 6422560 | tf_op jit(solution)/shard_map/all_to_all | solution.py:84
  295.8 4.8 fusion.1
  300.6 5.2 fusion.4
  305.9 7.3 copy.34
  313.1 14.3 %convert_element_type.67 = bf16[448,7168]{1,0:T(8,128)(2,1)} reshape(bf16[1,448,32,224]{3,2,1,0:T(8,128)(2,1)} %copy.34) | data formatting | bytes 12845056 | tf_op jit(solution)/shard_map/convert_element_type | solution.py:90
  327.5 5.7 fusion.9
  333.2 16.4 %convolution_bitcast_fusion = f32[1,448,7168]{2,1,0:T(8,128)} fusion(bf16[1,256,7168]{2,1,0:T(8,128)(2,1)} %param.25, bf16[448,7168]{1,0:T(8,128)(2,1)} %convert_element_type.67, bf16[1,7168,256]{2,1,0:T(8,128)(2,1)} %param.24, f32[448,256]{1,0:T(8,128)S(1)} %fusion.9), kind=kOutput, calls=%fused_computation.9 | convolution fusion | flops 3289022464 | bytes 27066368 | tf_op jit(solution)/shard_map/dot_general | solution.py:94
  349.6 31.8 %copy.35 = f32[1,448,7168]{1,0,2:T(1,128)} copy(f32[1,448,7168]{2,1,0:T(8,128)} %convolution_bitcast_fusion) | data formatting | bytes 25690112 | tf_op jit(solution)/shard_map/broadcast_in_dim | solution.py:95
  381.4 25.1 %all-to-all-start.1 = ((f32[1,448,7168]{1,0,2:T(1,128)}), f32[1,448,7168]{1,0,2:T(1,128)}, u32[]{:S(2)}, u32[]{:S(2)}) async-start(f32[1,448,7168]{1,0,2:T(1,128)} %copy.35), calls=%async_computation.1 | async-start | bytes 29360128 | tf_op jit(solution)/shard_map/all_to_all | solution.py:95
  406.7 195.8 %all-to-all-done.1 = f32[1,448,7168]{1,0,2:T(1,128)} async-done(((f32[1,448,7168]{1,0,2:T(1,128)}), f32[1,448,7168]{1,0,2:T(1,128)}, u32[]{:S(2)}, u32[]{:S(2)}) %all-to-all-start.1) | async-done | bytes 12845088 | tf_op jit(solution)/shard_map/all_to_all | solution.py:95
  602.5 30.3 %copy.36 = f32[1,448,32,224]{3,1,2,0:T(8,128)} copy(f32[1,448,32,224]{1,0,3,2:T(1,128)} %bitcast.13) | data formatting | bytes 25690112 | tf_op jit(solution)/shard_map/all_to_all | solution.py:95
  632.8 10.5 %concatenate.7 = f32[14337,224]{1,0:T(8,128)} pad(f32[14336,224]{1,0:T(8,128)} %bitcast.73, f32[]{:T(128)} %constant.22.clone.1), padding=0_1x0_0 | pad | bytes 25691012 | tf_op jit(solution)/shard_map/concatenate | solution.py:98
  643.3 29.1 %gather_fusion.1 = f32[6144,224]{1,0:T(8,128)} fusion(f32[14337,224]{1,0:T(8,128)} %concatenate.7, s32[6144]{0:T(1024)S(1)} %broadcast_clamp_fusion.1), kind=kCustom, calls=%fused_computation.1 | custom fusion | bytes 11034624 | tf_op jit(solution)/shard_map/gather | solution.py:99
  672.4 7.0 fusion.5
  679.4 72.3 %reduce-scatter.4.cloned.1.call-done = f32[96,224]{1,0:T(8,128)} async-done(((f32[768,224]{1,0:T(8,128)}), f32[96,224]{1,0:T(8,128)}) %reduce-scatter.4.cloned.1.call-update) | async-done | bytes 86032
  (54 shorter events, 9.4 us)
Async XLA Ops:
  6.5 4.2 copy-start
  6.5 17.1 %copy-start.4 = (s32[768,8]{0,1:T(8,128)S(1)}, s32[768,8]{0,1:T(8,128)}, u32[]{:S(2)}) copy-start(s32[768,8]{0,1:T(8,128)} %param.20) | copy-start | bytes 73732
  6.5 17.8 %copy-start.7 = (s32[32]{0:T(128)S(1)}, s32[32]{0:T(128)}, u32[]{:S(2)}) copy-start(s32[32]{0:T(128)} %param.22) | copy-start | bytes 388
  6.5 55.9 %copy-start.2 = (bf16[1024,224]{0,1:T(8,128)(2,1)S(1)}, bf16[1024,224]{0,1:T(8,128)(2,1)}, u32[]{:S(2)}) copy-start(bf16[1024,224]{0,1:T(8,128)(2,1)} %param.17) | copy-start | bytes 1376260
  6.5 55.9 %all-gather.2.cloned.1.call-start = ((), (), s32[]{:S(2)}) async-start(), calls=%async_computation.3 | async-start | bytes 1622016 | tf_op jit(solution)/shard_map/all_gather | solution.py:73
  10.7 129.1 %copy-start.3 = (bf16[768,224]{0,1:T(8,128)(2,1)S(1)}, bf16[768,224]{0,1:T(8,128)(2,1)}, u32[]{:S(2)}) copy-start(bf16[768,224]{0,1:T(8,128)(2,1)} %param.18) | copy-start | bytes 1032196
  11.7 128.2 %all-reduce.4.cloned.1.call-start = ((), (), s32[]{:S(2)}) async-start(), calls=%async_computation.4 | async-start | bytes 1376256 | tf_op jit(solution)/shard_map/psum | solution.py:77
  198.2 7.6 %copy-start.5 = (f32[7168]{0:T(1024)S(1)}, f32[7168]{0:T(1024)}, u32[]{:S(2)}) copy-start(f32[7168]{0:T(1024)} %param.19) | copy-start | bytes 86020
  198.2 97.6 %all-to-all-start = ((bf16[32,448,224]{2,1,0:T(8,128)(2,1)}), bf16[32,448,224]{2,1,0:T(8,128)(2,1)}, u32[]{:S(2)}, u32[]{:S(2)}) async-start(bf16[32,448,224]{2,1,0:T(8,128)(2,1)} %bitcast.74), calls=%async_computation | async-start | bytes 14680064 | tf_op jit(solution)/shard_map/all_to_all | solution.py:84
  381.4 25.1 %copy-start.6 = (f32[768,8]{0,1:T(8,128)S(1)}, f32[768,8]{0,1:T(8,128)}, u32[]{:S(2)}) copy-start(f32[768,8]{0,1:T(8,128)} %param.21) | copy-start | bytes 73732
  381.4 221.1 %all-to-all-start.1 = ((f32[1,448,7168]{1,0,2:T(1,128)}), f32[1,448,7168]{1,0,2:T(1,128)}, u32[]{:S(2)}, u32[]{:S(2)}) async-start(f32[1,448,7168]{1,0,2:T(1,128)} %copy.35), calls=%async_computation.1 | async-start | bytes 29360128 | tf_op jit(solution)/shard_map/all_to_all | solution.py:95
  406.4 345.3 %reduce-scatter.4.cloned.1.call-start = ((), (), s32[]{:S(2)}) async-start(), calls=%async_computation.5 | async-start | bytes 884736
  643.3 110.2 %copy-start.1 = (bf16[8,512,128]{2,1,0:T(8,128)(2,1)S(1)}, bf16[8,512,128]{2,1,0:T(8,128)(2,1)}, u32[]{:S(2)}) copy-start(bf16[8,512,128]{2,1,0:T(8,128)(2,1)} %param.16) | copy-start | bytes 3145732
Sparse Core Ops, SparseCore 0:
  11.8 50.5 all-gather.1
  65.5 74.3 all-reduce.3
  679.5 72.1 reduce-scatter.3
where the time goes:
time: 763 us; the launch traced here: 760 us
  waiting for transfers between devices  447 us (59%)
  local copies, waits for them, and re-layouts  209 us (27%)
  starting transfers between devices  32.8 us (4%)
  other arithmetic  29.9 us (4%)
  matrix products  28.4 us (4%)
  between operations  13.4 us (2%)
    all_to_all x1, waiting for transfers between devices, shards(): lax.all_to_all(expert_part[None], 'expert', split_axis=2, concat_axis=0,...  196 us
    all_to_all x1, waiting for transfers between devices, shards(): lax.all_to_all(outgoing, 'expert', split_axis=0, concat_axis=2, tiled=True)  89.9 us
    unnamed x4, waiting for transfers between devices  72.4 us
    gather x1, local copies, waits for them, and re-layouts, shards(): outgoing = padded[slot_row]  56.9 us
    psum x1, waiting for transfers between devices, shards(): attention = lax.psum(partial_out, 'tensor')  51.2 us
    all_gather x1, waiting for transfers between devices, shards(): lax.all_gather(head_rows, 'expert', axis=0, tiled=True)  37.6 us
    broadcast_in_dim x1, local copies, waits for them, and re-layouts, shards(): expert_part[None]  31.8 us
    all_to_all x1, local copies, waits for them, and re-layouts, shards(): lax.all_to_all(expert_part[None], 'expert', split_axis=2, concat_axis=0,...  30.3 us
  transfers between devices with their start and end apart: 5, of which 5 were waited for; matrix products, arithmetic and copies ran while one was open for 5% of the time, Pallas kernels for 0%

commit v1 on v0

v1 whole, which is shorter than its diff:
```python
import jax
import jax.numpy as jnp
from jax import lax
from jax.sharding import PartitionSpec as P

ROTARY_CHANNELS = 64
NOPE = 128
SIDE = 4
CORES = 2

epsilon = 1e-06


def place(x, y, core):
    return (x * SIDE + y) * CORES + core


def ring_groups():
    along_y = [[place(x, y, 0) for y in range(SIDE)] for x in range(SIDE)]
    along_x = [[place(x, y, 0) for x in range(SIDE)] for y in range(SIDE)]
    along_y1 = [[place(x, y, 1) for y in range(SIDE)] for x in range(SIDE)]
    along_x1 = [[place(x, y, 1) for x in range(SIDE)] for y in range(SIDE)]
    inner = along_y + along_x1
    outer = along_x + along_y1
    pairs = [[place(x, y, 0), place(x, y, 1)] for x in range(SIDE) for y in range(SIDE)]
    return inner, outer, pairs


INNER, OUTER, PAIRS = ring_groups()


def exchange(blocks, groups):
    return lax.all_to_all(blocks, "expert", 0, 0, axis_index_groups=groups, tiled=True)


def spread(block, groups, count):
    return exchange(jnp.broadcast_to(block[None], (count,) + block.shape), groups)


def gather_plane(block):
    block = spread(block, INNER, SIDE)
    block = spread(block, OUTER, SIDE)
    return spread(block, PAIRS, CORES)


def add_blocks(blocks):
    return jnp.sum(blocks.astype(jnp.float32), axis=0)


def plane_order(table):
    tail = table.shape[1:]
    cube = table.reshape((SIDE, SIDE, CORES) + tail)
    return jnp.stack([cube[:, :, 0], jnp.swapaxes(cube[:, :, 1], 0, 1)])


def row_order(table):
    return jnp.stack([table[0], jnp.swapaxes(table[1], 0, 1)], axis=2)


def shards(
    queries,
    latent_cache_rows,
    lengths,
    value_up_weight,
    w_output,
    residual,
    norm_gain,
    routes,
    gate_values,
    capacity,
    w_gate,
    w_up,
    w_down,
):
    latent_width = value_up_weight.shape[1]
    softmax_scale = (NOPE + ROTARY_CHANNELS) ** (-0.5)
    scores = (
        jnp.einsum("rhc,rpc->rhp", queries, latent_cache_rows, preferred_element_type=jnp.float32)
        * softmax_scale
    )
    slot_total = latent_cache_rows.shape[1]
    live_slot = lax.broadcasted_iota(jnp.int32, (1, 1, slot_total), 2) < lengths[:, None, None]
    scores = jnp.where(live_slot, scores, -jnp.inf)
    row_peak = jnp.max(scores, axis=-1, keepdims=True)
    weight_exp = jnp.exp(scores - row_peak)
    attention_probs = (weight_exp / jnp.sum(weight_exp, axis=-1, keepdims=True)).astype(
        jnp.bfloat16
    )
    latent_rows = jnp.einsum(
        "onq,oqv->onv",
        attention_probs,
        latent_cache_rows[:, :, :latent_width],
        preferred_element_type=jnp.float32,
    ).astype(jnp.bfloat16)
    head_out = jnp.einsum(
        "rhc,hcv->rhv", latent_rows, value_up_weight, preferred_element_type=jnp.float32
    ).astype(jnp.bfloat16)
    head_rows = head_out.reshape(head_out.shape[0], -1)

    expert = lax.axis_index("expert")
    layer = lax.axis_index("tensor")
    layers = lax.axis_size("tensor")
    row_total, column_width = residual.shape
    own_rows = row_total // layers
    model_width = norm_gain.shape[0]
    hidden = w_gate.shape[2]

    named = routes == expert
    member = jnp.any(named, axis=1)
    gate_of = jnp.sum(jnp.where(named, gate_values, 0.0), axis=1)
    earlier = jnp.arange(row_total)[:, None] > jnp.arange(row_total)[None, :]
    position = jnp.dot(
        earlier.astype(jnp.bfloat16),
        member.astype(jnp.bfloat16),
        preferred_element_type=jnp.float32,
    )
    limit = capacity[expert].astype(jnp.float32)
    row_weight = jnp.where(position < limit, gate_of, 0.0)

    gate_up = jnp.concatenate([w_gate[0], w_up[0]], axis=1)
    gate_up = plane_order(gate_up.reshape(-1, column_width, 2 * hidden))
    gate_up = gate_up.reshape(model_width, 2 * hidden)
    down = plane_order(w_down[0].T.reshape(-1, column_width, hidden))
    down = down.reshape(model_width, hidden)
    gain = plane_order(norm_gain.reshape(-1, column_width)).reshape(model_width, 1)

    heads = gather_plane(head_rows)
    partial_out = jnp.dot(
        heads.reshape(row_total, -1), w_output, preferred_element_type=jnp.float32
    )
    partial_out = partial_out.reshape(CORES, SIDE, SIDE, -1, column_width)
    partial_out = row_order(partial_out).reshape(layers, own_rows, column_width)
    attention = add_blocks(
        lax.all_to_all(partial_out.astype(jnp.bfloat16), "tensor", 0, 0, tiled=True)
    )
    own_residual = lax.dynamic_slice_in_dim(residual, layer * own_rows, own_rows, 0)
    stream = (own_residual.astype(jnp.float32) + attention).astype(jnp.bfloat16)
    columns = lax.all_to_all(
        jnp.broadcast_to(stream[None], (layers,) + stream.shape), "tensor", 0, 0, tiled=True
    )
    columns = columns.reshape(row_total, column_width).T

    full = gather_plane(columns).reshape(model_width, row_total)
    as_float = full.astype(jnp.float32)
    scale = lax.rsqrt(jnp.mean(as_float * as_float, axis=0, keepdims=True) + epsilon)
    normed = (as_float * scale * gain).astype(jnp.bfloat16)
    pre = lax.dot_general(
        gate_up, normed, (((0,), (0,)), ((), ())), preferred_element_type=jnp.float32
    )
    activated = (jax.nn.silu(pre[:hidden]) * pre[hidden:]).astype(jnp.bfloat16)
    produced = jnp.dot(down, activated, preferred_element_type=jnp.float32)
    weighted = (produced * row_weight[None, :]).astype(jnp.bfloat16)

    parts = weighted.reshape(CORES, SIDE, SIDE, column_width, row_total)
    parts = add_blocks(exchange(parts, PAIRS)).astype(jnp.bfloat16)
    parts = add_blocks(exchange(parts, OUTER)).astype(jnp.bfloat16)
    parts = add_blocks(exchange(parts, INNER)).astype(jnp.bfloat16)
    parts = parts.T.reshape(layers, own_rows, column_width)
    combined = add_blocks(lax.all_to_all(parts, "tensor", 0, 0, tiled=True))
    return (stream.astype(jnp.float32) + combined).astype(jnp.bfloat16)


def solution(mesh):
    in_specs = (
        P("expert", "tensor", None),
        P("expert", None, None),
        P("expert"),
        P("tensor", None, None),
        P("tensor", "expert"),
        P(None, "expert"),
        P(),
        P(),
        P(),
        P(),
        P("expert", None, "tensor"),
        P("expert", None, "tensor"),
        P("expert", "tensor", None),
    )
    out_specs = P("tensor", "expert")
    return jax.shard_map(shards, mesh=mesh, in_specs=in_specs, out_specs=out_specs, check_vma=False)
```

time: 763 us -> 275 us (0.36)
  waiting for transfers between devices: 447 us -> 27.6 us
  local copies, waits for them, and re-layouts: 209 us -> 26.2 us
  blocking collectives: 0 us -> 161 us
  starting transfers between devices: 32.8 us -> 15.1 us
  between operations: 13.4 us -> 0.95 us
  matrix products: 28.4 us -> 20.5 us
    all_to_all x2, waiting for transfers between devices: 286 us -> 27.6 us  [the longest x1 13.9 us: shards(): lax.all_to_all(partial_out.astype(jnp.bfloat16), 'tensor', 0, 0, tiled=True)]
    all_to_all x0 -> x10, blocking collectives: none -> 161 us  [the longest x8 127 us: exchange(): lax.all_to_all(blocks, 'expert', 0, 0, axis_index_groups=groups, tiled=True)]
    gather x2 -> x0, local copies, waits for them, and re-layouts: 85.9 us -> none  [the longest x1 56.9 us: shards(): outgoing = padded[slot_row]]
    unnamed x4 -> x0, waiting for transfers between devices: 72.4 us -> none
    psum x1 -> x0, waiting for transfers between devices: 51.2 us -> none  [shards(): attention = lax.psum(partial_out, 'tensor')]
    all_gather x1 -> x0, waiting for transfers between devices: 37.6 us -> none  [shards(): lax.all_gather(head_rows, 'expert', axis=0, tiled=True)]
    all_to_all x1 -> x0, local copies, waits for them, and re-layouts: 30.3 us -> none  [shards(): lax.all_to_all(expert_part[None], 'expert', split_axis=2, concat_axis=0,...]
    broadcast_in_dim x1 -> x8, local copies, waits for them, and re-layouts: 31.8 us -> 7.97 us  [the longest x7 7.94 us: spread(): jnp.broadcast_to(block[None], (count,) + block.shape)]
  transfers between devices with their start and end apart: 5 -> 2, of which waited for: 5 -> 2; matrix products, arithmetic and copies ran while one was open for 5% -> 6% of each run, Pallas kernels for 0% -> 0%
where the time goes in v1:
time: 275 us; the launch traced here: 274 us
  blocking collectives  161 us (59%)
  waiting for transfers between devices  27.6 us (10%)
  local copies, waits for them, and re-layouts  26.2 us (10%)
  other arithmetic  22.5 us (8%)
  matrix products  20.5 us (7%)
  starting transfers between devices  15.1 us (5%)
    all_to_all x8, blocking collectives, exchange(): lax.all_to_all(blocks, 'expert', 0, 0, axis_index_groups=groups, tiled=True)  127 us
    all_to_all x1, blocking collectives, shards(): lax.all_to_all(jnp.broadcast_to(stream[None], (layers,) + stream.shape),...  17.5 us
    all_to_all x1, blocking collectives, shards(): combined = add_blocks(lax.all_to_all(parts, 'tensor', 0, 0, tiled=True))  16 us
    reduce_sum x5, other arithmetic, add_blocks(): return jnp.sum(blocks.astype(jnp.float32), axis=0)  15.3 us
    all_to_all x1, waiting for transfers between devices, shards(): lax.all_to_all(partial_out.astype(jnp.bfloat16), 'tensor', 0, 0, tiled=True)  13.9 us
    all_to_all x1, waiting for transfers between devices, exchange(): lax.all_to_all(blocks, 'expert', 0, 0, axis_index_groups=groups, tiled=True)  13.7 us
    dot_general x1, matrix products, shards(): lax.dot_general(gate_up, normed, (((0,), (0,)), ((), ())), preferred_elem...  10.5 us
    unnamed x22, local copies, waits for them, and re-layouts  8.9 us
  transfers between devices with their start and end apart: 2, of which 2 were waited for; matrix products, arithmetic and copies ran while one was open for 6% of the time, Pallas kernels for 0%

profile of v1, /device:TPU:2, one launch (start us, length us, event | category | flops | bytes accessed | tf_op | source)
XLA Modules:
  0.0 273.5 jit_solution(2539285755197691357)
XLA Ops:
  4.5 10.6 %all_to_all.60 = bf16[4,24,1024]{2,1,0:T(8,128)(2,1)S(1)} all-to-all(bf16[4,24,1024]{2,1,0:T(8,128)(2,1)S(1)} %broadcast_in_dim.39), channel_id=1, replica_groups={{0,2,4,6},{8,10,12,14},{16,18,20,22},{24,26,28,30},{1,9,17,25},{3,11,19..., dimensions={0} | all-to-all | bytes 393216 | tf_op jit(solution)/shard_map/all_to_all | solution.py:33
  15.2 12.8 %all_to_all.61 = bf16[4,4,24,1024]{3,2,1,0:T(8,128)(2,1)S(1)} all-to-all(bf16[4,4,24,1024]{3,2,1,0:T(8,128)(2,1)S(1)} %broadcast_in_dim.40), channel_id=1, replica_groups={{0,8,16,24},{2,10,18,26},{4,12,20,28},{6,14,22,30},{1,3,5,7},{9,11,13,1..., dimensions={0} | all-to-all | bytes 1572864 | tf_op jit(solution)/shard_map/all_to_all | solution.py:33
  28.2 5.0 %all_to_all.62 = bf16[2,4,4,24,1024]{4,3,2,1,0:T(8,128)(2,1)S(1)} all-to-all(bf16[2,4,4,24,1024]{4,3,2,1,0:T(8,128)(2,1)S(1)} %broadcast_in_dim.41), channel_id=1, replica_groups={{0,1},{2,3},{4,5},{6,7},{8,9},{10,11},{12,13},{14,15},{16,17},{18,19},{..., dimensions={0} | all-to-all | bytes 3145728 | tf_op jit(solution)/shard_map/all_to_all | solution.py:33
  35.1 8.5 %all-to-all-start.3 = ((bf16[8,96,224]{2,1,0:T(8,128)(2,1)}), bf16[8,96,224]{2,1,0:T(8,128)(2,1)S(1)}, u32[]{:S(2)}, u32[]{:S(2)}) async-start(bf16[8,96,224]{2,1,0:T(8,128)(2,1)} %bitcast.6), calls=%async_computation.3 | async-start | bytes 786432 | tf_op jit(solution)/shard_map/all_to_all | solution.py:134
  44.6 13.9 %all-to-all-done.3 = bf16[8,96,224]{2,1,0:T(8,128)(2,1)S(1)} async-done(((bf16[8,96,224]{2,1,0:T(8,128)(2,1)}), bf16[8,96,224]{2,1,0:T(8,128)(2,1)S(1)}, u32[]{:S(2)}, u32[]{:S(2)}) %all-to-all-start.3) | async-done | bytes 344096 | tf_op jit(solution)/shard_map/all_to_all | solution.py:134
  58.6 17.5 %all_to_all.63 = bf16[8,96,224]{2,1,0:T(8,128)(2,1)S(1)} all-to-all(bf16[8,96,224]{2,1,0:T(8,128)(2,1)S(1)} %broadcast_in_dim.42), channel_id=1, replica_groups=mesh['tensor'=8,'expert'=32] {'tensor'}, dimensions={0} | all-to-all | bytes 688128 | tf_op jit(solution)/shard_map/all_to_all | solution.py:138
  76.4 15.1 %all_to_all.64 = bf16[4,224,768]{2,1,0:T(8,128)(2,1)S(1)} all-to-all(bf16[4,224,768]{2,1,0:T(8,128)(2,1)S(1)} %broadcast_in_dim.43), channel_id=1, replica_groups={{0,2,4,6},{8,10,12,14},{16,18,20,22},{24,26,28,30},{1,9,17,25},{3,11,19..., dimensions={0} | all-to-all | bytes 2752512 | tf_op jit(solution)/shard_map/all_to_all | solution.py:33
  91.5 3.0 %broadcast_in_dim.44 = bf16[4,4,224,768]{3,2,1,0:T(8,128)(2,1)} broadcast(bf16[4,224,768]{2,1,0:T(8,128)(2,1)S(1)} %all_to_all.64), dimensions={1,2,3} | broadcast | bytes 6881280 | tf_op jit(solution)/shard_map/broadcast_in_dim | solution.py:37
  94.5 6.6 %all-to-all-start.6 = ((bf16[4,4,224,768]{3,2,1,0:T(8,128)(2,1)}), bf16[4,4,224,768]{3,2,1,0:T(8,128)(2,1)}, u32[]{:S(2)}, u32[]{:S(2)}) async-start(bf16[4,4,224,768]{3,2,1,0:T(8,128)(2,1)} %broadcast_in_dim.44), calls=%async_computation.6 | async-start | bytes 11010048 | tf_op jit(solution)/shard_map/all_to_all | solution.py:33
  102.6 5.9 %copy.41 = bf16[1,256,7168]{1,2,0:T(8,128)(2,1)} copy(bf16[1,256,7168]{2,1,0:T(8,128)(2,1)} %param.25) | data formatting | bytes 7340032 | tf_op args[12]
  108.6 2.3 slice_bitcast_fusion.1
  117.0 3.7 %copy_bitcast_fusion = (bf16[1,4,4,224,512]{4,3,2,1,0:T(8,128)(2,1)}, bf16[1,4,4,224,512]{4,3,1,2,0:T(8,128)(2,1)}) fusion(bf16[4,4,1,224,512]{4,3,2,1,0:T(8,128)(2,1)S(1)} %get-tuple-element.8, bf16[4,4,1,224,512]{4,3,2,1,0:T(8,128)(2,1)S(1)} %get-tuple-element.7), kind=kLoop, calls=%fused_computation.18 | loop fusion | bytes 14680064 | tf_op jit(solution)/shard_map/stack | solution.py:53
  120.8 13.7 %all-to-all-done.6 = bf16[4,4,224,768]{3,2,1,0:T(8,128)(2,1)} async-done(((bf16[4,4,224,768]{3,2,1,0:T(8,128)(2,1)}), bf16[4,4,224,768]{3,2,1,0:T(8,128)(2,1)}, u32[]{:S(2)}, u32[]{:S(2)}) %all-to-all-start.6) | async-done | bytes 5505056 | tf_op jit(solution)/shard_map/all_to_all | solution.py:33
  134.5 4.6 %broadcast_in_dim.45 = bf16[2,4,4,224,768]{4,3,2,1,0:T(8,128)(2,1)S(1)} broadcast(bf16[4,4,224,768]{3,2,1,0:T(8,128)(2,1)} %all-to-all-done.6), dimensions={1,2,3,4} | broadcast | bytes 16515072 | tf_op jit(solution)/shard_map/broadcast_in_dim | solution.py:37
  139.1 12.6 %all_to_all.65 = bf16[2,4,4,224,768]{4,3,2,1,0:T(8,128)(2,1)S(1)} all-to-all(bf16[2,4,4,224,768]{4,3,2,1,0:T(8,128)(2,1)S(1)} %broadcast_in_dim.45), channel_id=1, replica_groups={{0,1},{2,3},{4,5},{6,7},{8,9},{10,11},{12,13},{14,15},{16,17},{18,19},{..., dimensions={0} | all-to-all | bytes 22020096 | tf_op jit(solution)/shard_map/all_to_all | solution.py:33
  151.7 2.5 fusion.1
  154.2 10.5 %fusion.13 = f32[512,768]{1,0:T(8,128)} fusion(bf16[2,4,4,224,768]{4,3,2,1,0:T(8,128)(2,1)S(1)} %all_to_all.65, f32[2,4,4,224]{3,2,1,0:T(4,128)S(1)} %copy.48, f32[768]{0:T(1024)S(1)} %add_rsqrt_fusion, bf16[1,4,4,224,512]{4,3,2,1,0:T(8,128)(2,1)} %get-tuple-element.15, bf16[1,4,4,224,512]{4,3,1,2,0:T(8,128)(2,1)} %get-tuple-element.16), kind=kOutput, calls=%fused_computation.25 | convolution fusion | flops 5673844736 | bytes 19954688 | tf_op jit(solution)/shard_map/dot_general | solution.py:147
  164.7 5.6 %multiply_convert_fusion = bf16[7168,768]{1,0:T(8,128)(2,1)S(1)} fusion(bf16[7168,256]{1,0:T(8,128)(2,1)} %bitcast.75, f32[768]{0:T(1024)S(1)} %compare_select_fusion, f32[512,768]{1,0:T(8,128)} %fusion.13), kind=kOutput, calls=%fused_computation.6 | convolution fusion | flops 2830761984 | bytes 16256000 | tf_op jit(solution)/shard_map/dot_general | solution.py:151
  170.3 14.1 %all_to_all.66 = bf16[2,4,4,224,768]{4,3,2,1,0:T(8,128)(2,1)} all-to-all(bf16[2,4,4,224,768]{4,3,2,1,0:T(8,128)(2,1)S(1)} %bitcast.71), channel_id=1, replica_groups={{0,1},{2,3},{4,5},{6,7},{8,9},{10,11},{12,13},{14,15},{16,17},{18,19},{..., dimensions={0} | all-to-all | bytes 22020096 | tf_op jit(solution)/shard_map/all_to_all | solution.py:33
  184.3 9.9 %reduce_sum.85 = bf16[4,4,224,768]{3,2,1,0:T(8,128)(2,1)} reduce(bf16[2,4,4,224,768]{4,3,2,1,0:T(8,128)(2,1)} %all_to_all.66, bf16[]{:T(256)} %constant.36.clone.1), dimensions={0}, to_apply=%region_6.7 | reduce | flops 2752512 | bytes 16515074 | tf_op jit(solution)/shard_map/reduce_sum | solution.py:47
  194.2 40.9 %all_to_all.67 = bf16[4,4,224,768]{3,2,1,0:T(8,128)(2,1)} all-to-all(bf16[4,4,224,768]{3,2,1,0:T(8,128)(2,1)} %reduce_sum.85), channel_id=1, replica_groups={{0,8,16,24},{2,10,18,26},{4,12,20,28},{6,14,22,30},{1,3,5,7},{9,11,13,1..., dimensions={0} | all-to-all | bytes 11010048 | tf_op jit(solution)/shard_map/all_to_all | solution.py:33
  235.1 5.0 %reduce_sum.86 = bf16[4,224,768]{2,1,0:T(8,128)(2,1)} reduce(bf16[4,4,224,768]{3,2,1,0:T(8,128)(2,1)} %all_to_all.67, bf16[]{:T(256)} %constant.36.clone.1), dimensions={0}, to_apply=%region_7.8 | reduce | flops 2064384 | bytes 6881282 | tf_op jit(solution)/shard_map/reduce_sum | solution.py:47
  240.1 16.2 %all_to_all.68 = bf16[4,224,768]{2,1,0:T(8,128)(2,1)S(1)} all-to-all(bf16[4,224,768]{2,1,0:T(8,128)(2,1)} %reduce_sum.86), channel_id=1, replica_groups={{0,2,4,6},{8,10,12,14},{16,18,20,22},{24,26,28,30},{1,9,17,25},{3,11,19..., dimensions={0} | all-to-all | bytes 2752512 | tf_op jit(solution)/shard_map/all_to_all | solution.py:33
  256.8 16.0 %all_to_all.69 = bf16[8,96,224]{2,1,0:T(8,128)(2,1)S(1)} all-to-all(bf16[8,96,224]{2,1,0:T(8,128)(2,1)S(1)} %bitcast.78), channel_id=1, replica_groups=mesh['tensor'=8,'expert'=32] {'tensor'}, dimensions={0} | all-to-all | bytes 688128 | tf_op jit(solution)/shard_map/all_to_all | solution.py:159
  (61 shorter events, 16.2 us)
Async XLA Ops:
  0.0 4.1 %copy-start = (bf16[8,512,128]{2,1,0:T(8,128)(2,1)S(1)}, bf16[8,512,128]{2,1,0:T(8,128)(2,1)}, u32[]{:S(2)}) copy-start(bf16[8,512,128]{2,1,0:T(8,128)(2,1)} %param.16) | copy-start | bytes 3145732
  15.2 18.0 %copy-start.7 = (bf16[1024,224]{0,1:T(8,128)(2,1)S(1)}, bf16[1024,224]{0,1:T(8,128)(2,1)}, u32[]{:S(2)}) copy-start(bf16[1024,224]{0,1:T(8,128)(2,1)} %param.17) | copy-start | bytes 1376260
  35.1 23.5 %all-to-all-start.3 = ((bf16[8,96,224]{2,1,0:T(8,128)(2,1)}), bf16[8,96,224]{2,1,0:T(8,128)(2,1)S(1)}, u32[]{:S(2)}, u32[]{:S(2)}) async-start(bf16[8,96,224]{2,1,0:T(8,128)(2,1)} %bitcast.6), calls=%async_computation.3 | async-start | bytes 786432 | tf_op jit(solution)/shard_map/all_to_all | solution.py:134
  94.5 6.6 %copy-start.4 = (f32[7168]{0:T(1024)S(1)}, f32[7168]{0:T(1024)}, u32[]{:S(2)}) copy-start(f32[7168]{0:T(1024)} %param.19) | copy-start | bytes 86020
  94.5 6.8 %copy-start.8 = (s32[32]{0:T(128)S(1)}, s32[32]{0:T(128)}, u32[]{:S(2)}) copy-start(s32[32]{0:T(128)} %param.22) | copy-start | bytes 388
  94.5 8.1 %copy-start.5 = (s32[768,8]{0,1:T(8,128)S(1)}, s32[768,8]{0,1:T(8,128)}, u32[]{:S(2)}) copy-start(s32[768,8]{0,1:T(8,128)} %param.20) | copy-start | bytes 73732
  94.5 40.0 %all-to-all-start.6 = ((bf16[4,4,224,768]{3,2,1,0:T(8,128)(2,1)}), bf16[4,4,224,768]{3,2,1,0:T(8,128)(2,1)}, u32[]{:S(2)}, u32[]{:S(2)}) async-start(bf16[4,4,224,768]{3,2,1,0:T(8,128)(2,1)} %broadcast_in_dim.44), calls=%async_computation.6 | async-start | bytes 11010048 | tf_op jit(solution)/shard_map/all_to_all | solution.py:33
  110.9 0.7 copy-start.6
  112.0 3.4 %copy-start.2 = (bf16[1,7168,256]{2,1,0:T(8,128)(2,1)S(1)}, bf16[1,7168,256]{2,1,0:T(8,128)(2,1)}, u32[]{:S(2)}) copy-start(bf16[1,7168,256]{2,1,0:T(8,128)(2,1)} %param.23) | copy-start | bytes 11010052
  112.0 4.5 %copy-start.3 = (bf16[1,7168,256]{2,1,0:T(8,128)(2,1)S(1)}, bf16[1,7168,256]{2,1,0:T(8,128)(2,1)}, u32[]{:S(2)}) copy-start(bf16[1,7168,256]{2,1,0:T(8,128)(2,1)} %param.24) | copy-start | bytes 11010052
  235.1 38.4 %copy-start.1 = (bf16[8,512,128]{2,1,0:T(8,128)(2,1)S(1)}, bf16[8,512,128]{2,1,0:T(8,128)(2,1)}, u32[]{:S(2)}) copy-start(bf16[8,512,128]{2,1,0:T(8,128)(2,1)} %param.16) | copy-start | bytes 3145732
